TPU v7x, 256 devices: a whole 4x4x8 slice. The times are simulated.
256 devices in a mesh: rows: 4 (over y), coarse: 4 (over x_lo, core), fine: 16 (over z, x_hi).
Axes of the slice: x: 4 (x_hi: 2, x_lo: 2; x = x_hi * 2 + x_lo), y: 4, z: 8, core: 2. Of those that a mesh axis runs over, the one named last changes fastest.
Arguments:
- eigvecs: bfloat16 [2048, 32768], P('rows', ('coarse', 'fine')), may hold values from -6 to 6
- perm: int32 [32768], P(('coarse', 'fine')), may hold values from 0 to 511, as said below
- counts: int32 [64], replicated, may hold values from 1 to 256, as said below
- poles: float32 [32768], replicated, may hold values from 0 to 32768, as said below
- weights: float32 [32768], replicated, may hold values from -10 to 10, as said below
- roots: float32 [32768], P(('coarse', 'fine')), may hold values from 0 to 32768, as said below
Outputs:
- merged: bfloat16 [2048, 32768], P('rows', ('coarse', 'fine'))
Inputs may be any that keep to these rules, and one draw needn't show every extreme that they name: `perm`: each aligned block of 512 entries is a permutation of 0 to 511. `counts`: at least one device has exactly 256. Every entry of poles lies 0.2 or more away from every entry of roots. `weights`: magnitudes 0.1 or more. `roots`: every entry lies 0.2 or more away from every entry of poles.
All inputs are finite; a program needn't handle non-finite values.
Results may differ from a plain program's by a relative error of at most 0.0027.
Values may be sent and summed in bfloat16 or wider, within the bound.
No kernel may reach another device: no remote copies, remote signals or barrier semaphores. Data moves between devices by JAX's collectives and lax.ppermute only.
A program may use at most 64 MiB of HBM per device.

v0:
```python
import jax
import jax.numpy as jnp
from jax import lax
from jax.sharding import PartitionSpec as P

UNDEF_MOST = 256


def per_device(eigvecs, perm, counts, poles, weights, roots):
    columns_dev = eigvecs.shape[1]
    live_width = UNDEF_MOST
    device_total = counts.shape[0]
    n_coarse = lax.axis_size("coarse")
    n_fine = lax.axis_size("fine")
    device_ids = jnp.arange(device_total, dtype=jnp.int32)
    my_device = lax.axis_index("coarse") * n_fine + lax.axis_index("fine")
    my_count = jnp.sum(jnp.where(device_ids == my_device, counts, 0))
    column_ids = jnp.arange(columns_dev, dtype=jnp.int32)
    selector = (column_ids[:, None] == perm[None, :]).astype(jnp.bfloat16)
    permuted = jnp.dot(eigvecs, selector, preferred_element_type=jnp.float32).astype(jnp.bfloat16)
    own_roots = roots[:live_width]
    outgoing = permuted[:, :live_width]
    within = jnp.arange(live_width, dtype=jnp.int32)
    alive = within[None, :] < counts[:, None]
    factor_table = jnp.where(alive, weights.reshape(device_total, columns_dev)[:, :live_width], 0.0)
    pole_table = poles.reshape(device_total, columns_dev)[:, :live_width]
    factor_flat = jnp.transpose(
        factor_table.reshape(n_coarse, n_fine, live_width), (1, 0, 2)
    ).reshape(-1)
    pole_flat = jnp.transpose(pole_table.reshape(n_coarse, n_fine, live_width), (1, 0, 2)).reshape(
        -1
    )
    panels = lax.all_gather(outgoing, "coarse", axis=1, tiled=True)
    panel_piece = lax.all_gather(panels, "fine", axis=1, tiled=True)
    cauchy = factor_flat[:, None] / (pole_flat[:, None] - own_roots[None, :])
    summed = jnp.dot(panel_piece, cauchy.astype(jnp.bfloat16), preferred_element_type=jnp.float32)
    summed, squares = (summed, jnp.sum(cauchy * cauchy, axis=0))
    updated = summed / jnp.sqrt(squares)[None, :]
    retain = within < my_count
    leading = jnp.where(retain[None, :], updated, outgoing.astype(jnp.float32)).astype(jnp.bfloat16)
    return jnp.concatenate([leading, permuted[:, live_width:]], axis=1)


def solution(mesh):
    in_specs = (
        P("rows", ("coarse", "fine")),
        P(("coarse", "fine")),
        P(),
        P(),
        P(),
        P(("coarse", "fine")),
    )
    out_specs = P("rows", ("coarse", "fine"))
    return jax.shard_map(
        per_device, mesh=mesh, in_specs=in_specs, out_specs=out_specs, check_vma=False
    )
```

profile of v0, /device:TPU:1, one launch (start us, length us, event | category | flops | bytes accessed | tf_op | source)
XLA Modules:
  0.0 287.3 jit_solution(11880553413928689479)
XLA Ops:
  6.5 0.0 copy-start
  6.5 0.0 all-gather.3.cloned.1.call-start
  6.5 1.0 copy-done
  7.6 1.2 fusion.6
  8.8 0.7 fusion.20
  9.5 0.0 all-gather.3.cloned.1.call-update
  9.5 0.0 all-gather.5.cloned.1.call-start
  9.6 27.6 %all-gather.3.cloned.1.call-done = bf16[512,1024]{0,1:T(8,128)(2,1)} async-done(((bf16[512,256]{0,1:T(8,128)(2,1)}), bf16[512,1024]{0,1:T(8,128)(2,1)}) %all-gather.3.cloned.1.call-update) | async-done | bytes 1048592 | tf_op jit(solution)/shard_map/all_gather | solution.py:33
  37.1 0.0 all-gather.5.cloned.1.call-update
  37.1 0.7 slice.18
  37.8 0.9 reshape.26
  38.9 0.9 reshape.24
  39.8 0.7 slice_select_fusion
  40.6 9.0 %multiply_reduce_fusion = f32[256]{0:T(256)S(1)} fusion(f32[256]{0:T(256)S(1)} %slice.18, f32[16384]{0:T(1024)S(1)} %bitcast.18, f32[16384]{0:T(1024)S(1)} %bitcast.20), kind=kLoop, calls=%fused_computation | loop fusion | flops 16776960 | bytes 133120 | tf_op jit(solution)/shard_map/reduce_sum | solution.py:37
  49.7 1.3 fusion.19
  51.0 0.6 iota_compare_fusion.2
  51.6 213.3 %all-gather.5.cloned.1.call-done = bf16[512,16384]{0,1:T(8,128)(2,1)} async-done(((bf16[512,1024]{0,1:T(8,128)(2,1)}), bf16[512,16384]{0,1:T(8,128)(2,1)}) %all-gather.5.cloned.1.call-update) | async-done | bytes 16777232 | tf_op jit(solution)/shard_map/all_gather | solution.py:34
  264.9 14.5 %fusion.13 = bf16[512,256]{0,1:T(8,128)(2,1)S(1)} fusion(bf16[512,16384]{0,1:T(8,128)(2,1)} %all-gather.5.cloned.1.call-done, f32[256]{0:T(256)S(1)} %slice.18, f32[16384]{0:T(1024)S(1)} %bitcast.19, f32[16384]{0:T(1024)S(1)} %bitcast.21, f32[256]{0:T(256)S(1)} %sqrt.7, pred[256]{0:T(512)(128)(4,1)S(1)} %iota_compare_fusion.2, bf16[512,512]{0,1:T(8,128)(2,1)S(1)} %fusion.6), kind=kOutput, calls=%fused_computation.11 | convolution fusion | flops 4308074496 | bytes 17434880 | tf_op jit(solution)/shard_map/dot_general | solution.py:36
  279.5 1.0 copy.14
  (7 shorter events, 0.2 us)
Async XLA Ops:
  6.5 1.0 copy-start
  6.5 30.6 %all-gather.3.cloned.1.call-start = ((), (), s32[]{:S(2)}) async-start(), calls=%async_computation | async-start | bytes 1310720 | tf_op jit(solution)/shard_map/all_gather | solution.py:33
  9.5 255.4 %all-gather.5.cloned.1.call-start = ((), (), s32[]{:S(2)}) async-start(), calls=%async_computation.1 | async-start | bytes 17825792 | tf_op jit(solution)/shard_map/all_gather | solution.py:34
Sparse Core Ops, SparseCore 0:
  9.6 27.4 all-gather.2
  39.7 225.1 all-gather.4
where the time goes:
time: 288 us; the launch traced here: 287 us
  waiting for transfers between devices  241 us (84%)
  matrix products  15.7 us (5%)
  between operations  13.5 us (5%)
  other arithmetic  11.7 us (4%)
  local copies, waits for them, and re-layouts  5.5 us (2%)
    all_gather x1, waiting for transfers between devices, per_device(): panel_piece = lax.all_gather(panels, 'fine', axis=1, tiled=True)  213 us
    all_gather x1, waiting for transfers between devices, per_device(): panels = lax.all_gather(outgoing, 'coarse', axis=1, tiled=True)  27.6 us
    dot_general x1, matrix products, per_device(): jnp.dot(panel_piece, cauchy.astype(jnp.bfloat16), preferred_element_type=...  14.5 us
    reduce_sum x1, other arithmetic, per_device(): summed, squares = (summed, jnp.sum(cauchy * cauchy, axis=0))  9.01 us
  transfers between devices with their start and end apart: 2, of which 2 were waited for; matrix products, arithmetic and copies ran while one was open for 5% of the time, Pallas kernels for 0%

commit v1 on v0

--- a/solution.py
+++ b/solution.py
@@ -30,7 +30,9 @@
     pole_flat = jnp.transpose(pole_table.reshape(n_coarse, n_fine, live_width), (1, 0, 2)).reshape(
         -1
     )
-    panels = lax.all_gather(outgoing, "coarse", axis=1, tiled=True)
+    panels = jnp.concatenate(
+        lax.all_to_all(jnp.stack([outgoing] * lax.axis_size("coarse")), "coarse", 0, 0), axis=1
+    )
     panel_piece = lax.all_gather(panels, "fine", axis=1, tiled=True)
     cauchy = factor_flat[:, None] / (pole_flat[:, None] - own_roots[None, :])
     summed = jnp.dot(panel_piece, cauchy.astype(jnp.bfloat16), preferred_element_type=jnp.float32)

time: 288 us -> 278 us (0.965)
  waiting for transfers between devices: 241 us -> 212 us
  blocking collectives: 0 us -> 19.8 us
    all_gather x1 -> x0, waiting for transfers between devices: 27.6 us -> none  [per_device(): panels = lax.all_gather(outgoing, 'coarse', axis=1, tiled=True)]
    all_to_all x0 -> x1, blocking collectives: none -> 19.8 us  [per_device(): lax.all_to_all(jnp.stack([outgoing] * lax.axis_size('coarse')), 'coarse',...]
  transfers between devices with their start and end apart: 2 -> 1, of which waited for: 2 -> 1; matrix products, arithmetic and copies ran while one was open for 5% -> 5% of each run, Pallas kernels for 0% -> 0%
where the time goes in v1:
time: 278 us; the launch traced here: 277 us
  waiting for transfers between devices  212 us (76%)
  blocking collectives  19.8 us (7%)
  matrix products  15.7 us (6%)
  between operations  13.5 us (5%)
  other arithmetic  11.7 us (4%)
  local copies, waits for them, and re-layouts  4.88 us (2%)
    all_gather x1, waiting for transfers between devices, per_device(): panel_piece = lax.all_gather(panels, 'fine', axis=1, tiled=True)  212 us
    all_to_all x1, blocking collectives, per_device(): lax.all_to_all(jnp.stack([outgoing] * lax.axis_size('coarse')), 'coarse',...  19.8 us
    dot_general x1, matrix products, per_device(): jnp.dot(panel_piece, cauchy.astype(jnp.bfloat16), preferred_element_type=...  14.5 us
    reduce_sum x1, other arithmetic, per_device(): summed, squares = (summed, jnp.sum(cauchy * cauchy, axis=0))  9.01 us
  transfers between devices with their start and end apart: 1, of which 1 were waited for; matrix products, arithmetic and copies ran while one was open for 5% of the time, Pallas kernels for 0%

profile of v1, /device:TPU:1, one launch (start us, length us, event | category | flops | bytes accessed | tf_op | source)
XLA Modules:
  0.0 277.5 jit_solution(8673869450973481017)
XLA Ops:
  6.5 0.0 copy-start
  6.5 0.0 all-gather.2.cloned.1.call-start
  6.5 1.0 copy-done
  7.6 1.2 fusion.6
  8.8 0.1 stack.2
  8.9 19.8 %all_to_all.5 = bf16[4,512,256]{1,2,0:T(8,128)(2,1)} all-to-all(bf16[4,512,256]{1,2,0:T(8,128)(2,1)S(1)} %stack.2), channel_id=1, replica_groups=mesh['rows'=4,'coarse'=4,'fine'=16] {'coarse'}, dimensions={0} | all-to-all | bytes 2097152 | tf_op jit(solution)/shard_map/all_to_all | solution.py:34
  28.7 0.0 all-gather.2.cloned.1.call-update
  28.7 0.7 slice.18
  29.4 0.9 reshape.36
  30.4 0.9 reshape.34
  31.4 0.7 slice_select_fusion
  32.2 9.0 %multiply_reduce_fusion = f32[256]{0:T(256)S(1)} fusion(f32[256]{0:T(256)S(1)} %slice.18, f32[16384]{0:T(1024)S(1)} %bitcast.22, f32[16384]{0:T(1024)S(1)} %bitcast.24), kind=kLoop, calls=%fused_computation | loop fusion | flops 16776960 | bytes 133120 | tf_op jit(solution)/shard_map/reduce_sum | solution.py:39
  41.2 1.3 fusion.19
  42.5 0.7 iota_compare_fusion.2
  43.2 211.9 %all-gather.2.cloned.1.call-done = bf16[512,16384]{0,1:T(8,128)(2,1)} async-done(((bf16[512,1024]{0,1:T(8,128)(2,1)}), bf16[512,16384]{0,1:T(8,128)(2,1)}) %all-gather.2.cloned.1.call-update) | async-done | bytes 16777232 | tf_op jit(solution)/shard_map/all_gather | solution.py:36
  255.1 14.5 %fusion.13 = bf16[512,256]{0,1:T(8,128)(2,1)S(1)} fusion(bf16[512,16384]{0,1:T(8,128)(2,1)} %all-gather.2.cloned.1.call-done, f32[256]{0:T(256)S(1)} %slice.18, f32[16384]{0:T(1024)S(1)} %bitcast.23, f32[16384]{0:T(1024)S(1)} %bitcast.25, f32[256]{0:T(256)S(1)} %sqrt.7, pred[256]{0:T(512)(128)(4,1)S(1)} %iota_compare_fusion.2, bf16[512,512]{0,1:T(8,128)(2,1)S(1)} %fusion.6), kind=kOutput, calls=%fused_computation.11 | convolution fusion | flops 4308074496 | bytes 17434880 | tf_op jit(solution)/shard_map/dot_general | solution.py:38
  269.6 1.0 copy.15
  (8 shorter events, 0.2 us)
Async XLA Ops:
  6.5 1.0 copy-start
  6.5 248.6 %all-gather.2.cloned.1.call-start = ((), (), s32[]{:S(2)}) async-start(), calls=%async_computation.1 | async-start | bytes 17825792 | tf_op jit(solution)/shard_map/all_gather | solution.py:36
Sparse Core Ops, SparseCore 0:
  28.8 226.2 all-gather.1
